TPU v7x, 32 devices: a whole 2x2x4 slice. The times are simulated.
32 devices in a mesh: groups: 2 (over x), req: 8 (over z, y), head: 2 (over core).
Axes of the slice: x: 2, y: 2, z: 4, core: 2. Of those that a mesh axis runs over, the one named last changes fastest.
Arguments:
- queries: bfloat16 [2048, 32, 128], P(('groups', 'req'), 'head'), parts along dimension 0, may hold values from -100 to 100
- new_keys: bfloat16 [2048, 2, 128], P(('groups', 'req'), 'head'), parts along dimension 0, may hold values from -4.5 to 4.5
- new_values: bfloat16 [2048, 2, 128], P(('groups', 'req'), 'head'), parts along dimension 0, may hold values from -6 to 6
- cluster_kv: bfloat16 [1024, 2, 2, 128, 128], P(('groups', 'req'), 'head'), parts along dimension 0, may hold values from -6 to 6
- cluster_len: int32 [32], P('groups'), parts along dimension 0, may hold values from 1 to 4096, 40960 in all
- piece_slot: int32 [32, 32], P('groups'), parts along dimension 0, may hold values from 0 to 511, as said below
- cluster_ids: int32 [16, 2, 2], P('groups', 'head'), parts along dimension 0, may hold values from 0 to 15, all different within a row
- w_out: bfloat16 [4096, 4096], P('head', 'req'), may hold values from -0.09375 to 0.09375
Outputs:
- projected: bfloat16 [2048, 4096], P(('groups', 'req', 'head')), parts along dimension 0
There are 2 independent parts, one for each index of `groups`. A program takes and returns all parts, laid end to end along the dimension named above; an argument that names none is the same for every part. Nothing has to cross between parts.
Inputs may be any that keep to these rules, and one draw needn't show every extreme that they name: `cluster_ids`: for each request and KV head, 2 distinct cluster numbers. A permutation of the slots: piece p of cluster c lies in slot piece_slot[c, p], stored on index slot // 64 of req, and every cluster has exactly 4 of its pieces on every index of req.
All inputs are finite; a program needn't handle non-finite values.
Results may differ from a plain program's by a relative error of at most 0.0052.
Values may be sent and summed in bfloat16 or wider, within the bound.
A program may use at most 128 MiB of HBM per device.

v0:
```python
import jax
import jax.numpy as jnp
from jax import lax
from jax.sharding import PartitionSpec as P


def local(queries, new_keys, new_values, cluster_kv, cluster_len, piece_slot, cluster_ids, w_out):
    my_index = lax.axis_index("req")
    peers = lax.axis_size("req")
    tok_rows = queries.shape[0]
    head_count = queries.shape[1]
    head_size = queries.shape[2]
    held_slots = cluster_kv.shape[0]
    piece_keys = cluster_kv.shape[3]
    pieces = piece_slot.shape[1]
    per_peer = pieces // peers
    scale_factor = head_size ** (-0.5)
    plan_rows = cluster_ids[:, 0, :]
    owner_of = piece_slot // held_slots
    local_of = piece_slot % held_slots
    piece_pos = jnp.arange(pieces, dtype=jnp.int32)
    earlier = piece_pos[:, None] > piece_pos[None, :]
    rank_of = jnp.sum(
        ((owner_of[:, :, None] == owner_of[:, None, :]) & earlier[None]).astype(jnp.int32), axis=2
    )
    rank_choice = jnp.arange(per_peer, dtype=jnp.int32)
    held_here = (
        (owner_of == my_index)[:, :, None] & (rank_of[:, :, None] == rank_choice[None, None, :])
    ).astype(jnp.int32)
    send_table = jnp.sum(held_here * local_of[:, :, None], axis=1)
    send_slots = send_table[plan_rows]
    outgoing = cluster_kv[:, 0][send_slots]
    incoming = lax.all_to_all(outgoing, "req", split_axis=0, concat_axis=0, tiled=True)
    my_plan = lax.dynamic_index_in_dim(plan_rows, my_index, 0, keepdims=False)
    my_owner = owner_of[my_plan]
    my_rank = rank_of[my_plan]
    peer_pos = jnp.arange(peers, dtype=jnp.int32)
    matches = (my_owner[None, :, None, :] == peer_pos[:, None, None, None]) & (
        my_rank[None, :, None, :] == rank_choice[None, None, :, None]
    )
    piece_at = jnp.sum(matches.astype(jnp.int32) * piece_pos[None, None, None, :], axis=3)
    fill_limit = cluster_len[my_plan]
    key_pos = jnp.arange(piece_keys, dtype=jnp.int32)
    valid_keys = (
        piece_at[:, :, :, None] * piece_keys + key_pos[None, None, None, :]
        < fill_limit[None, :, None, None]
    ).reshape(-1)
    cached_keys = incoming[:, :, :, 0].reshape(-1, head_size)
    cached_values = incoming[:, :, :, 1].reshape(-1, head_size)
    position = jnp.arange(tok_rows, dtype=jnp.int32)
    causal = position[:, None] >= position[None, :]
    own_keys = new_keys[:, 0]
    own_values = new_values[:, 0]
    head_block = min(head_count, max(1, 512 // tok_rows))
    block_count = head_count // head_block
    causal_rows = jnp.tile(causal, (head_block, 1))

    def one_block(block_index):
        query_rows = lax.dynamic_slice_in_dim(queries, block_index * head_block, head_block, 1)
        query_rows = jnp.transpose(query_rows, (1, 0, 2)).reshape(head_block * tok_rows, head_size)
        cached_scores = (
            jnp.dot(query_rows, cached_keys.T, preferred_element_type=jnp.float32) * scale_factor
        )
        cached_scores = jnp.where(valid_keys[None, :], cached_scores, -jnp.inf)
        own_scores = (
            jnp.dot(query_rows, own_keys.T, preferred_element_type=jnp.float32) * scale_factor
        )
        own_scores = jnp.where(causal_rows, own_scores, -jnp.inf)
        row_top = jnp.maximum(jnp.max(cached_scores, axis=1), jnp.max(own_scores, axis=1))
        cached_weights = jnp.exp(cached_scores - row_top[:, None])
        own_weights = jnp.exp(own_scores - row_top[:, None])
        row_total = jnp.sum(cached_weights, axis=1) + jnp.sum(own_weights, axis=1)
        mixed_sum = jnp.dot(
            cached_weights.astype(jnp.bfloat16), cached_values, preferred_element_type=jnp.float32
        )
        mixed_sum = mixed_sum + jnp.dot(
            own_weights.astype(jnp.bfloat16), own_values, preferred_element_type=jnp.float32
        )
        result = (mixed_sum / row_total[:, None]).astype(jnp.bfloat16)
        return result.reshape(head_block, tok_rows, head_size)

    attended = lax.map(one_block, jnp.arange(block_count, dtype=jnp.int32)).reshape(
        head_count, tok_rows, head_size
    )
    segment = lax.all_gather(w_out, "req", axis=1, tiled=True)
    shaped = segment.reshape(head_count, head_size, segment.shape[1])
    head_terms = jnp.einsum("htd,hdn->tn", attended, shaped, preferred_element_type=jnp.float32)
    projected = lax.psum_scatter(head_terms, "head", scatter_dimension=0, tiled=True).astype(
        jnp.bfloat16
    )
    return projected


def solution(mesh):
    return jax.shard_map(
        local,
        mesh=mesh,
        in_specs=(
            P(("groups", "req"), "head", None),
            P(("groups", "req"), "head", None),
            P(("groups", "req"), "head", None),
            P(("groups", "req"), "head", None, None, None),
            P("groups"),
            P("groups", None),
            P("groups", "head", None),
            P("head", "req"),
        ),
        out_specs=P(("groups", "req", "head"), None),
        check_vma=False,
    )
```

profile of v0, /device:TPU:4, one launch (start us, length us, event | category | flops | bytes accessed | tf_op | source)
XLA Modules:
  0.0 352.0 jit_solution(10308188675530318257)
XLA Ops:
  6.5 0.7 all-gather.2.cloned.1.call-update
  7.3 0.7 broadcast_compare_fusion
  8.5 0.7 add_select_fusion
  9.4 0.7 compare_select_fusion.1
  11.0 5.2 %gather_fusion.4 = bf16[64,2,128,128]{3,2,1,0:T(8,128)(2,1)} fusion(bf16[64,2,128,128]{3,2,1,0:T(8,128)(2,1)} %bitcast.67, s32[1024]{0:T(1024)S(1)} %pad_clamp_fusion.1), kind=kCustom, calls=%fused_computation.4 | custom fusion | bytes 8388864 | tf_op jit(solution)/shard_map/gather | solution.py:32
  16.2 5.1 %copy.25 = bf16[8,2,4,2,128,128]{5,4,2,1,3,0:T(8,128)(2,1)} copy(bf16[8,2,4,2,128,128]{5,4,3,2,1,0:T(8,128)(2,1)} %bitcast.64) | data formatting | bytes 8388608 | tf_op jit(solution)/shard_map/gather | solution.py:32
  21.3 6.4 %all-to-all-start = ((bf16[8,2,4,2,128,128]{5,4,2,1,3,0:T(8,128)(2,1)}), bf16[8,2,4,2,128,128]{5,4,2,1,3,0:T(8,128)(2,1)}, u32[]{:S(2)}, u32[]{:S(2)}) async-start(bf16[8,2,4,2,128,128]{5,4,2,1,3,0:T(8,128)(2,1)} %copy.25), calls=%async_computation | async-start | bytes 8388608 | tf_op jit(solution)/shard_map/all_to_all | solution.py:33
  29.4 0.6 gather_fusion.2
  30.0 178.4 %all-to-all-done = bf16[8,2,4,2,128,128]{5,4,2,1,3,0:T(8,128)(2,1)} async-done(((bf16[8,2,4,2,128,128]{5,4,2,1,3,0:T(8,128)(2,1)}), bf16[8,2,4,2,128,128]{5,4,2,1,3,0:T(8,128)(2,1)}, u32[]{:S(2)}, u32[]{:S(2)}) %all-to-all-start) | async-done | bytes 4194336 | tf_op jit(solution)/shard_map/all_to_all | solution.py:33
  208.5 4.0 %fusion.24 = (bf16[8,2,4,1,128,128]{5,4,2,1,3,0:T(8,128)(2,1)}, bf16[8,2,4,1,128,128]{5,4,2,1,3,0:T(8,128)(2,1)S(1)}) fusion(bf16[8,2,4,2,128,128]{5,4,2,1,3,0:T(8,128)(2,1)} %all-to-all-done), kind=kLoop, calls=%fused_computation.57 | loop fusion | bytes 8388608 | tf_op jit(solution)/shard_map/slice | solution.py:49
  212.5 113.6 %while.11 = (s32[]{:T(128)}, bf16[4,4,128,128]{3,2,1,0:T(8,128)(2,1)S(1)}, s32[4]{0:T(128)S(1)}, bf16[128,16,128]{2,1,0:T(8,128)(2,1)}, bf16[8192,128]{1,0:T(8,1...) while((s32[]{:T(128)}, ...), condition=%wide.region_8.9_spmd.clone, body=%wide.region_3.8_spmd.clone.sunk | while | flops 2227846144 | bytes 57293268 | solution.py:82
  212.5 0.6 dynamic_slice.19
  213.7 1.0 constant_dynamic-slice_fusion.2
  214.8 7.1 %fusion.55 = (f32[512]{0:T(512)S(1)}, f32[512,8192]{1,0:T(8,128)}) fusion(pred[8192]{0:T(1024)(128)(4,1)S(1)} %bitcast.69, bf16[512,128]{1,0:T(8,128)(2,1)S(1)} %bitcast.65, bf16[8192,128]{1,0:T(8,128)(2,1)S(1)} %get-tuple-element.269), kind=kOutput, calls=%fused_computation.9.clone.1 | convolution fusion | flops 1086324224 | bytes 19015680 | tf_op jit(solution)/shard_map/while/body/eval_jaxpr/dot_general | solution.py:62
  222.3 9.8 %fusion.58 = f32[512]{0:T(512)S(1)} fusion(f32[512,8192]{1,0:T(8,128)} %get-tuple-element.231, f32[512]{0:T(512)S(1)} %max.9, pred[8192]{0:T(1024)(128)(4,1)S(1)} %bitcast.70), kind=kLoop, calls=%fused_computation.10.clone.1 | loop fusion | flops 16776704 | bytes 16789504 | tf_op jit(solution)/shard_map/while/body/eval_jaxpr/reduce_sum | solution.py:72
  232.1 8.4 %fusion.57 = f32[512,128]{1,0:T(8,128)S(1)} fusion(bf16[8192,128]{1,0:T(8,128)(2,1)} %get-tuple-element.271, f32[512,8192]{1,0:T(8,128)} %get-tuple-element.231, f32[512]{0:T(512)S(1)} %max.9, pred[8192]{0:T(1024)(128)(4,1)S(1)} %bitcast.71), kind=kOutput, calls=%fused_computation.12.clone.1 | convolution fusion | flops 1090519040 | bytes 19146752 | tf_op jit(solution)/shard_map/while/body/eval_jaxpr/dot_general | solution.py:73
  240.8 0.6 dynamic_slice.19
  242.0 1.0 constant_dynamic-slice_fusion.2
  243.1 7.1 %fusion.55 = (f32[512]{0:T(512)S(1)}, f32[512,8192]{1,0:T(8,128)}) fusion(pred[8192]{0:T(1024)(128)(4,1)S(1)} %bitcast.69, bf16[512,128]{1,0:T(8,128)(2,1)S(1)} %bitcast.65, bf16[8192,128]{1,0:T(8,128)(2,1)S(1)} %get-tuple-element.269), kind=kOutput, calls=%fused_computation.9.clone.1 | convolution fusion | flops 1086324224 | bytes 19015680 | tf_op jit(solution)/shard_map/while/body/eval_jaxpr/dot_general | solution.py:62
  250.6 9.9 %fusion.58 = f32[512]{0:T(512)S(1)} fusion(f32[512,8192]{1,0:T(8,128)} %get-tuple-element.231, f32[512]{0:T(512)S(1)} %max.9, pred[8192]{0:T(1024)(128)(4,1)S(1)} %bitcast.70), kind=kLoop, calls=%fused_computation.10.clone.1 | loop fusion | flops 16776704 | bytes 16789504 | tf_op jit(solution)/shard_map/while/body/eval_jaxpr/reduce_sum | solution.py:72
  260.5 8.4 %fusion.57 = f32[512,128]{1,0:T(8,128)S(1)} fusion(bf16[8192,128]{1,0:T(8,128)(2,1)} %get-tuple-element.271, f32[512,8192]{1,0:T(8,128)} %get-tuple-element.231, f32[512]{0:T(512)S(1)} %max.9, pred[8192]{0:T(1024)(128)(4,1)S(1)} %bitcast.71), kind=kOutput, calls=%fused_computation.12.clone.1 | convolution fusion | flops 1090519040 | bytes 19146752 | tf_op jit(solution)/shard_map/while/body/eval_jaxpr/dot_general | solution.py:73
  270.4 1.0 constant_dynamic-slice_fusion.2
  271.6 7.3 %fusion.55 = (f32[512]{0:T(512)S(1)}, f32[512,8192]{1,0:T(8,128)}) fusion(pred[8192]{0:T(1024)(128)(4,1)S(1)} %bitcast.69, bf16[512,128]{1,0:T(8,128)(2,1)S(1)} %bitcast.65, bf16[8192,128]{1,0:T(8,128)(2,1)S(1)} %get-tuple-element.269), kind=kOutput, calls=%fused_computation.9.clone.1 | convolution fusion | flops 1086324224 | bytes 19015680 | tf_op jit(solution)/shard_map/while/body/eval_jaxpr/dot_general | solution.py:62
  279.2 9.9 %fusion.58 = f32[512]{0:T(512)S(1)} fusion(f32[512,8192]{1,0:T(8,128)} %get-tuple-element.231, f32[512]{0:T(512)S(1)} %max.9, pred[8192]{0:T(1024)(128)(4,1)S(1)} %bitcast.70), kind=kLoop, calls=%fused_computation.10.clone.1 | loop fusion | flops 16776704 | bytes 16789504 | tf_op jit(solution)/shard_map/while/body/eval_jaxpr/reduce_sum | solution.py:72
  289.2 8.4 %fusion.57 = f32[512,128]{1,0:T(8,128)S(1)} fusion(bf16[8192,128]{1,0:T(8,128)(2,1)} %get-tuple-element.271, f32[512,8192]{1,0:T(8,128)} %get-tuple-element.231, f32[512]{0:T(512)S(1)} %max.9, pred[8192]{0:T(1024)(128)(4,1)S(1)} %bitcast.71), kind=kOutput, calls=%fused_computation.12.clone.1 | convolution fusion | flops 1090519040 | bytes 19146752 | tf_op jit(solution)/shard_map/while/body/eval_jaxpr/dot_general | solution.py:73
  299.1 1.0 constant_dynamic-slice_fusion.2
  300.2 7.1 %fusion.55 = (f32[512]{0:T(512)S(1)}, f32[512,8192]{1,0:T(8,128)}) fusion(pred[8192]{0:T(1024)(128)(4,1)S(1)} %bitcast.69, bf16[512,128]{1,0:T(8,128)(2,1)S(1)} %bitcast.65, bf16[8192,128]{1,0:T(8,128)(2,1)S(1)} %get-tuple-element.269), kind=kOutput, calls=%fused_computation.9.clone.1 | convolution fusion | flops 1086324224 | bytes 19015680 | tf_op jit(solution)/shard_map/while/body/eval_jaxpr/dot_general | solution.py:62
  307.7 9.8 %fusion.58 = f32[512]{0:T(512)S(1)} fusion(f32[512,8192]{1,0:T(8,128)} %get-tuple-element.231, f32[512]{0:T(512)S(1)} %max.9, pred[8192]{0:T(1024)(128)(4,1)S(1)} %bitcast.70), kind=kLoop, calls=%fused_computation.10.clone.1 | loop fusion | flops 16776704 | bytes 16789504 | tf_op jit(solution)/shard_map/while/body/eval_jaxpr/reduce_sum | solution.py:72
  317.5 8.4 %fusion.57 = f32[512,128]{1,0:T(8,128)S(1)} fusion(bf16[8192,128]{1,0:T(8,128)(2,1)} %get-tuple-element.271, f32[512,8192]{1,0:T(8,128)} %get-tuple-element.231, f32[512]{0:T(512)S(1)} %max.9, pred[8192]{0:T(1024)(128)(4,1)S(1)} %bitcast.71), kind=kOutput, calls=%fused_computation.12.clone.1 | convolution fusion | flops 1090519040 | bytes 19146752 | tf_op jit(solution)/shard_map/while/body/eval_jaxpr/dot_general | solution.py:73
  326.2 8.5 %convolution_bitcast_fusion = f32[128,4096]{1,0:T(8,128)} fusion(bf16[16,128,128]{2,1,0:T(8,128)(2,1)S(1)} %bitcast.74, bf16[16,128,4096]{2,1,0:T(8,128)(2,1)} %bitcast.63), kind=kOutput, calls=%fused_computation.28 | convolution fusion | flops 2147483648 | bytes 19398656 | tf_op jit(solution)/shard_map/htd,hdn->tn/dot_general | solution.py:87
  334.7 8.4 %reduce-scatter.2.cloned.1.call-done = f32[64,4096]{1,0:T(8,128)} async-done(((f32[128,4096]{1,0:T(8,128)}), f32[64,4096]{1,0:T(8,128)}) %reduce-scatter.2.cloned.1.call-update) | async-done | bytes 1048592 | tf_op jit(solution)/shard_map/reduce_scatter | solution.py:88
  343.1 2.1 convert_element_type.18
  (74 shorter events, 7.3 us)
Async XLA Ops:
  6.5 22.8 %copy-start = (s32[16]{0:T(128)S(1)}, s32[16]{0:T(128)}, u32[]{:S(2)}) copy-start(s32[16]{0:T(128)} %param.14) | copy-start | bytes 196
  6.5 21.1 %copy-start.1 = (s32[8,1,2]{0,2,1:T(2,128)S(1)}, s32[8,1,2]{0,2,1:T(2,128)}, u32[]{:S(2)}) copy-start(s32[8,1,2]{0,2,1:T(2,128)} %param.16) | copy-start | bytes 196
  6.5 319.6 %all-gather.2.cloned.1.call-start = ((), (), s32[]{:S(2)}) async-start(), calls=%async_computation.2 | async-start | bytes 18874368 | tf_op jit(solution)/shard_map/all_gather | solution.py:85
  10.9 201.6 %copy-start.2 = (bf16[128,1,128]{2,0,1:T(8,128)(2,1)S(1)}, bf16[128,1,128]{2,0,1:T(8,128)(2,1)}, u32[]{:S(2)}) copy-start(bf16[128,1,128]{2,0,1:T(8,128)(2,1)} %param.11) | copy-start | bytes 98308
  11.0 201.5 %copy-start.3 = (bf16[128,1,128]{2,0,1:T(8,128)(2,1)S(1)}, bf16[128,1,128]{2,0,1:T(8,128)(2,1)}, u32[]{:S(2)}) copy-start(bf16[128,1,128]{2,0,1:T(8,128)(2,1)} %param.12) | copy-start | bytes 98308
  21.3 187.2 %all-to-all-start = ((bf16[8,2,4,2,128,128]{5,4,2,1,3,0:T(8,128)(2,1)}), bf16[8,2,4,2,128,128]{5,4,2,1,3,0:T(8,128)(2,1)}, u32[]{:S(2)}, u32[]{:S(2)}) async-start(bf16[8,2,4,2,128,128]{5,4,2,1,3,0:T(8,128)(2,1)} %copy.25), calls=%async_computation | async-start | bytes 8388608 | tf_op jit(solution)/shard_map/all_to_all | solution.py:33
  27.7 315.5 %reduce-scatter.2.cloned.1.call-start = ((), (), s32[]{:S(2)}) async-start(), calls=%async_computation.3 | async-start | bytes 3145728 | tf_op jit(solution)/shard_map/reduce_scatter | solution.py:88
Sparse Core Ops, SparseCore 0:
  9.4 310.0 all-gather.1
  334.8 8.2 reduce-scatter.1
where the time goes:
time: 354 us; the launch traced here: 352 us
  waiting for transfers between devices  188 us (53%)
  matrix products  72.5 us (20%)
  other arithmetic  45.2 us (13%)
  local copies, waits for them, and re-layouts  24.1 us (7%)
  between operations  13.5 us (4%)
  starting transfers between devices  6.43 us (2%)
    all_to_all x1, waiting for transfers between devices, local(): lax.all_to_all(outgoing, 'req', split_axis=0, concat_axis=0, tiled=True)  178 us
    reduce_sum x8, other arithmetic, one_block(): row_total = jnp.sum(cached_weights, axis=1) + jnp.sum(own_weights, axis=1)  39.7 us
    dot_general x4, matrix products, one_block(): jnp.dot(cached_weights.astype(jnp.bfloat16), cached_values, preferred_ele...  33.7 us
    dot_general x4, matrix products, one_block(): jnp.dot(query_rows, cached_keys.T, preferred_element_type=jnp.float32)  28.6 us
    gather x2, local copies, waits for them, and re-layouts, local(): outgoing = cluster_kv[:, 0][send_slots]  10.3 us
    dot_general x1, matrix products, local(): jnp.einsum('htd,hdn->tn', attended, shaped, preferred_element_type=jnp.fl...  8.49 us
    reduce_scatter x1, waiting for transfers between devices, local(): lax.psum_scatter(head_terms, 'head', scatter_dimension=0, tiled=True)  8.43 us
  transfers between devices with their start and end apart: 3, of which 2 were waited for; matrix products, arithmetic and copies ran while one was open for 37% of the time, Pallas kernels for 0%

commit v1 on v0

v1 whole, which is shorter than its diff:
```python
import functools

import jax
import jax.numpy as jnp
from jax import lax
from jax.experimental import pallas as pl
from jax.experimental.pallas import tpu as pltpu
from jax.sharding import PartitionSpec as P

MESH = pl.DeviceIdType.MESH
NEG = -1e30
LOG2E = 1.4426950408889634


def pick_kernel(peers, ids_ref, slot_ref, len_ref, kv_ref, send_ref, lim_ref, pick, count, sem):
    me = lax.axis_index("req")
    held, _, _, piece_keys, _ = kv_ref.shape
    sel = ids_ref.shape[1]
    pieces = slot_ref.shape[1]
    per = pieces // peers
    base = me * held

    @pl.loop(0, peers)
    def _(r):
        for s in range(sel):
            c = ids_ref[r, s]
            n = jnp.int32(0)
            for p in range(pieces):
                loc = slot_ref[c, p] - base
                pick[n] = loc
                n = n + ((loc >= 0) & (loc < held)).astype(jnp.int32)
            for j in range(per):
                pltpu.make_async_copy(kv_ref.at[pick[j], 0], send_ref.at[r, s * per + j], sem).start()

    for s in range(sel):
        c = ids_ref[me, s]
        fill = len_ref[c]
        for o in range(peers):
            count[o] = 0
        for p in range(pieces):
            o = slot_ref[c, p] // held
            j = count[o]
            lim_ref[o, s * per + j] = fill - p * piece_keys
            count[o] = j + 1
    pltpu.make_async_copy(send_ref, send_ref, sem).wait()


def attend_kernel(peers, heads, lim_ref, send_ref, q_ref, k_ref, v_ref, out_ref,
                  recv, qt, vt, top, total, acc, send_sem, recv_sem):
    me = lax.axis_index("req")
    tok = q_ref.shape[0]
    hd = k_ref.shape[1]
    count = send_ref.shape[1]
    piece_keys = send_ref.shape[3]
    rows = heads * tok
    block = min(256, rows)
    factor = hd ** (-0.5) * LOG2E

    barrier = pltpu.get_barrier_semaphore()
    for k in range(1, peers):
        pl.semaphore_signal(barrier, inc=1, device_id={"req": lax.rem(me + k, peers)}, device_id_type=MESH)
    pl.semaphore_wait(barrier, peers - 1)

    def peer_of(i):
        off = jnp.where(i % 2 == 1, (i + 1) // 2, peers - i // 2)
        return lax.rem(me + off, peers)

    def copy_to(peer):
        return pltpu.make_async_remote_copy(
            src_ref=send_ref.at[peer], dst_ref=recv.at[me],
            send_sem=send_sem.at[peer], recv_sem=recv_sem.at[me],
            device_id={"req": peer}, device_id_type=MESH)

    def copy_from(peer):
        return pltpu.make_async_remote_copy(
            src_ref=send_ref.at[peer], dst_ref=recv.at[peer],
            send_sem=send_sem.at[peer], recv_sem=recv_sem.at[peer],
            device_id={"req": peer}, device_id_type=MESH)

    @pl.loop(1, peers)
    def _(i):
        copy_to(peer_of(peers - i)).start()

    for h in range(heads):
        cols = slice(h * hd, (h + 1) * hd)
        qt[:, h * tok:(h + 1) * tok] = q_ref[:, cols].T
    own_vt = v_ref[...].T

    @pl.loop(0, rows // block)
    def _(b):
        cols = pl.ds(pl.multiple_of(b * block, block), block)
        s = jnp.dot(k_ref[...], qt[:, cols], preferred_element_type=jnp.float32)
        u = lax.broadcasted_iota(jnp.int32, s.shape, 0)
        t = lax.broadcasted_iota(jnp.int32, s.shape, 1) % tok
        s = jnp.where(u <= t, s, NEG)
        m = jnp.max(s, axis=0, keepdims=True)
        w = jnp.exp2((s - m) * factor)
        top[:, cols] = m
        total[:, cols] = jnp.sum(w, axis=0, keepdims=True)
        acc[:, cols] = jnp.dot(own_vt, w.astype(jnp.bfloat16), preferred_element_type=jnp.float32)

    def attend(src_ref, peer):
        for i in range(count):
            vt[:, i * piece_keys:(i + 1) * piece_keys] = src_ref[peer, i, 1].T

        @pl.loop(0, rows // block)
        def _(b):
            cols = pl.ds(pl.multiple_of(b * block, block), block)
            q = qt[:, cols]
            key = lax.broadcasted_iota(jnp.int32, (piece_keys, block), 0)
            m_old = top[:, cols]
            m = m_old
            scores = []
            for i in range(count):
                s = jnp.dot(src_ref[peer, i, 0], q, preferred_element_type=jnp.float32)
                s = jnp.where(key < lim_ref[peer, i], s, NEG)
                m = jnp.maximum(m, jnp.max(s, axis=0, keepdims=True))
                scores.append(s)
            keep = jnp.exp2((m_old - m) * factor)
            sums = total[:, cols] * keep
            low = []
            for s in scores:
                w = jnp.exp2((s - m) * factor)
                sums = sums + jnp.sum(w, axis=0, keepdims=True)
                low.append(w.astype(jnp.bfloat16))
            mixed = jnp.dot(vt[...], jnp.concatenate(low, axis=0), preferred_element_type=jnp.float32)
            top[:, cols] = m
            total[:, cols] = sums
            acc[:, cols] = acc[:, cols] * keep + mixed

    attend(send_ref, me)

    @pl.loop(1, peers)
    def _(i):
        peer = peer_of(i)
        copy_from(peer).wait_recv()
        attend(recv, peer)

    for h in range(heads):
        rows_h = slice(h * tok, (h + 1) * tok)
        o = acc[:, rows_h] / total[:, rows_h]
        out_ref[:, h * hd:(h + 1) * hd] = o.T.astype(out_ref.dtype)

    @pl.loop(1, peers)
    def _(i):
        copy_to(peer_of(i)).wait_send()


def local(queries, new_keys, new_values, cluster_kv, cluster_len, piece_slot, cluster_ids, w_out):
    peers = lax.axis_size("req")
    tok, heads, hd = queries.shape
    piece_keys = cluster_kv.shape[3]
    pieces = piece_slot.shape[1]
    sel = cluster_ids.shape[2]
    count = sel * (pieces // peers)
    vmem = pl.BlockSpec(memory_space=pltpu.VMEM)
    smem = pl.BlockSpec(memory_space=pltpu.SMEM)
    send, lim = pl.pallas_call(
        functools.partial(pick_kernel, peers),
        out_shape=(
            jax.ShapeDtypeStruct((peers, count, 2, piece_keys, hd), cluster_kv.dtype),
            jax.ShapeDtypeStruct((peers, count), jnp.int32),
        ),
        in_specs=[smem, smem, smem, pl.BlockSpec(memory_space=pl.ANY)],
        out_specs=(vmem, smem),
        scratch_shapes=[
            pltpu.SMEM((pieces + 1,), jnp.int32),
            pltpu.SMEM((peers,), jnp.int32),
            pltpu.SemaphoreType.DMA,
        ],
        name="pick",
    )(cluster_ids[:, 0, :], piece_slot, cluster_len, cluster_kv)
    rows = heads * tok
    attended = pl.pallas_call(
        functools.partial(attend_kernel, peers, heads),
        out_shape=jax.ShapeDtypeStruct((tok, heads * hd), jnp.bfloat16),
        in_specs=[smem, vmem, vmem, vmem, vmem],
        out_specs=vmem,
        scratch_shapes=[
            pltpu.VMEM((peers, count, 2, piece_keys, hd), cluster_kv.dtype),
            pltpu.VMEM((hd, rows), jnp.bfloat16),
            pltpu.VMEM((hd, count * piece_keys), jnp.bfloat16),
            pltpu.VMEM((1, rows), jnp.float32),
            pltpu.VMEM((1, rows), jnp.float32),
            pltpu.VMEM((hd, rows), jnp.float32),
            pltpu.SemaphoreType.DMA((peers,)),
            pltpu.SemaphoreType.DMA((peers,)),
        ],
        compiler_params=pltpu.CompilerParams(
            collective_id=0, has_side_effects=True, vmem_limit_bytes=40 * 2**20),
        name="attend",
    )(lim, send, queries.reshape(tok, heads * hd), new_keys[:, 0], new_values[:, 0])
    gathered = lax.all_gather(attended, "req", axis=0, tiled=True)
    terms = jnp.dot(gathered, w_out, preferred_element_type=jnp.float32)
    columns = w_out.shape[1]
    terms = terms.reshape(peers, tok, columns)
    summed = lax.psum_scatter(terms, "head", scatter_dimension=1, tiled=True).astype(jnp.bfloat16)
    mine = lax.all_to_all(summed, "req", split_axis=0, concat_axis=0, tiled=True)
    return jnp.transpose(mine, (1, 0, 2)).reshape(mine.shape[1], peers * columns)


def solution(mesh):
    return jax.shard_map(
        local,
        mesh=mesh,
        in_specs=(
            P(("groups", "req"), "head", None),
            P(("groups", "req"), "head", None),
            P(("groups", "req"), "head", None),
            P(("groups", "req"), "head", None, None, None),
            P("groups"),
            P("groups", None),
            P("groups", "head", None),
            P("head", "req"),
        ),
        out_specs=P(("groups", "req", "head"), None),
        check_vma=False,
    )
```

time: 354 us -> 278 us (0.79)
  Pallas kernels: 0 us -> 100 us
  matrix products: 72.5 us -> 5.83 us
  waiting for transfers between devices: 188 us -> 129 us
  other arithmetic: 45.2 us -> 1.29 us
  blocking collectives: 0 us -> 20.1 us
  local copies, waits for them, and re-layouts: 24.1 us -> 6.38 us
  starting transfers between devices: 6.43 us -> 0.04 us
    all_to_all x1 -> x0, waiting for transfers between devices: 178 us -> none  [local(): lax.all_to_all(outgoing, 'req', split_axis=0, concat_axis=0, tiled=True)]
    all_gather x1, waiting for transfers between devices: 0.02 us -> 119 us  [local(): gathered = lax.all_gather(attended, 'req', axis=0, tiled=True)]
    pallas_call x0 -> x2, Pallas kernels: none -> 100 us  [the longest x1 94.9 us: local(): pl.pallas_call(functools.partial(attend_kernel, peers, heads), out_shape=...]
    dot_general x17 -> x1, matrix products: 72.5 us -> 5.83 us  [local(): terms = jnp.dot(gathered, w_out, preferred_element_type=jnp.float32)]
    reduce_sum x11 -> x0, other arithmetic: 40.5 us -> none  [the longest x8 39.7 us: one_block(): row_total = jnp.sum(cached_weights, axis=1) + jnp.sum(own_weights, axis=1)]
    all_to_all x0 -> x1, blocking collectives: none -> 20.1 us  [local(): lax.all_to_all(summed, 'req', split_axis=0, concat_axis=0, tiled=True)]
    gather x6 -> x0, local copies, waits for them, and re-layouts: 12.6 us -> none  [the longest x2 10.3 us: local(): outgoing = cluster_kv[:, 0][send_slots]]
    dynamic_slice x13 -> x0, local copies, waits for them, and re-layouts: 6.7 us -> none  [the longest x8 4.19 us: one_block(): lax.dynamic_slice_in_dim(queries, block_index * head_block, head_block, 1)]
  transfers between devices with their start and end apart: 3 -> 2, of which waited for: 2 -> 2; matrix products, arithmetic and copies ran while one was open for 37% -> 0% of each run, Pallas kernels for 0% -> 0%
where the time goes in v1:
time: 278 us; the launch traced here: 276 us
  waiting for transfers between devices  129 us (46%)
  Pallas kernels  100 us (36%)
  blocking collectives  20.1 us (7%)
  between operations  13.5 us (5%)
  local copies, waits for them, and re-layouts  6.38 us (2%)
  matrix products  5.83 us (2%)
    all_gather x1, waiting for transfers between devices, local(): gathered = lax.all_gather(attended, 'req', axis=0, tiled=True)  119 us
    pallas_call x1, Pallas kernels, local(): pl.pallas_call(functools.partial(attend_kernel, peers, heads), out_shape=...  94.9 us
    all_to_all x1, blocking collectives, local(): lax.all_to_all(summed, 'req', split_axis=0, concat_axis=0, tiled=True)  20.1 us
    reduce_scatter x1, waiting for transfers between devices, local(): lax.psum_scatter(terms, 'head', scatter_dimension=1, tiled=True)  9.72 us
    dot_general x1, matrix products, local(): terms = jnp.dot(gathered, w_out, preferred_element_type=jnp.float32)  5.83 us
  transfers between devices with their start and end apart: 2, of which 2 were waited for; matrix products, arithmetic and copies ran while one was open for 0% of the time, Pallas kernels for 0%

profile of v1, /device:TPU:4, one launch (start us, length us, event | category | flops | bytes accessed | tf_op | source)
XLA Modules:
  0.0 276.5 jit_solution(9322276734448113055)
XLA Ops:
  6.5 0.0 copy-start
  6.5 0.0 copy-start.3
  6.5 0.0 copy-start.2
  6.5 0.0 all-gather.2.cloned.1.call-start
  6.5 1.5 copy.9.ids_ref
  8.0 1.2 copy.14
  9.2 5.5 %pick.1 = (bf16[8,8,2,128,128]{4,3,2,1,0:T(8,128)(2,1)}, s32[8,8]{1,0:T(8,128)}) custom-call(s32[8,2]{1,0:T(8,128)} %copy.9.ids_ref, s32[16,32]{1,0:T(8,128)} %slot_ref.1, s32[16]{0:T(128)} %len_ref.1, bf16[64,1,2,128,128]{4,3,2,1,0:T(8,128)(2,1)} %kv_ref.1), custom_call_target="tpu_custom_call" | custom-call | tf_op jit(solution)/shard_map/pick/pallas_call | solution.py:158
  14.8 0.0 copy-done.3
  14.8 0.0 copy-done.2
  14.8 0.0 copy-start.1
  14.8 2.2 copy-done.1
  17.0 0.0 copy-start.4
  17.0 0.7 copy-done.4
  17.7 94.9 %attend.1 = bf16[128,2048]{1,0:T(8,128)(2,1)} custom-call(s32[8,8]{1,0:T(8,128)S(1)} %copy-done.4, bf16[8,8,2,128,128]{4,3,2,1,0:T(8,128)(2,1)S(1)} %copy-done.1, bf16[128,2048]{1,0:T(8,128)(2,1)S(1)} %bitcast.13, bf16[128,128]{1,0:T(8,128)(2,1)S(1)} %bitcast.14, bf16[128,128]{1,0:T(8,128)(2,1)S(1)} %bitcast.15), custom_call_target="tpu_custom_call" | custom-call | tf_op jit(solution)/shard_map/attend/pallas_call | solution.py:174
  112.6 0.0 all-gather.2.cloned.1.call-update
  112.6 0.0 reduce-scatter.2.cloned.1.call-start
  112.7 119.1 %all-gather.2.cloned.1.call-done = bf16[1024,2048]{1,0:T(8,128)(2,1)} async-done(((bf16[128,2048]{1,0:T(8,128)(2,1)}), bf16[1024,2048]{1,0:T(8,128)(2,1)}) %all-gather.2.cloned.1.call-update) | async-done | bytes 4194320 | tf_op jit(solution)/shard_map/all_gather | solution.py:193
  231.8 0.0 copy-done
  231.8 5.8 %fusion = f32[1024,512]{1,0:T(8,128)} fusion(bf16[1024,2048]{1,0:T(8,128)(2,1)} %all-gather.2.cloned.1.call-done, bf16[2048,512]{1,0:T(8,128)(2,1)S(1)} %copy-done), kind=kOutput, calls=%fused_computation.1 | convolution fusion | flops 2147483648 | bytes 8388608 | tf_op jit(solution)/shard_map/dot_general | solution.py:194
  237.6 0.0 reduce-scatter.2.cloned.1.call-update
  237.7 9.7 %reduce-scatter.2.cloned.1.call-done = f32[8,64,512]{2,1,0:T(8,128)} async-done(((f32[8,128,512]{2,1,0:T(8,128)}), f32[8,64,512]{2,1,0:T(8,128)}) %reduce-scatter.2.cloned.1.call-update) | async-done | bytes 1048592 | tf_op jit(solution)/shard_map/reduce_scatter | solution.py:197
  247.4 1.3 convert_element_type.3
  248.7 20.1 %all_to_all.5 = bf16[8,64,512]{2,1,0:T(8,128)(2,1)S(1)} all-to-all(bf16[8,64,512]{2,1,0:T(8,128)(2,1)S(1)} %convert_element_type.3), channel_id=1, replica_groups=mesh['groups'=2,'req'=8,'head'=2] {'req'}, dimensions={0} | all-to-all | bytes 1048576 | tf_op jit(solution)/shard_map/all_to_all | solution.py:198
  268.8 0.8 copy.11
Async XLA Ops:
  6.5 225.3 %copy-start = (bf16[2048,512]{1,0:T(8,128)(2,1)S(1)}, bf16[2048,512]{1,0:T(8,128)(2,1)}, u32[]{:S(2)}) copy-start(bf16[2048,512]{1,0:T(8,128)(2,1)} %param.15) | copy-start | bytes 6291460
  6.5 8.2 %copy-start.3 = (bf16[128,1,128]{2,0,1:T(8,128)(2,1)S(1)}, bf16[128,1,128]{2,0,1:T(8,128)(2,1)}, u32[]{:S(2)}) copy-start(bf16[128,1,128]{2,0,1:T(8,128)(2,1)} %param.10) | copy-start | bytes 98308
  6.5 8.2 %copy-start.2 = (bf16[128,1,128]{2,0,1:T(8,128)(2,1)S(1)}, bf16[128,1,128]{2,0,1:T(8,128)(2,1)}, u32[]{:S(2)}) copy-start(bf16[128,1,128]{2,0,1:T(8,128)(2,1)} %param.9) | copy-start | bytes 98308
  6.5 225.3 %all-gather.2.cloned.1.call-start = ((), (), s32[]{:S(2)}) async-start(), calls=%async_computation.2 | async-start | bytes 4718592 | tf_op jit(solution)/shard_map/all_gather | solution.py:193
  14.8 2.2 copy-start.1
  17.0 0.7 copy-start.4
  112.6 134.8 %reduce-scatter.2.cloned.1.call-start = ((), (), s32[]{:S(2)}) async-start(), calls=%async_computation.3 | async-start | bytes 3145728 | tf_op jit(solution)/shard_map/reduce_scatter | solution.py:197
Sparse Core Ops, SparseCore 0:
  112.7 119.0 all-gather.1
  237.8 9.5 reduce-scatter.1

commit v2 on v1

--- a/solution.py
+++ b/solution.py
@@ -45,8 +45,8 @@
     pltpu.make_async_copy(send_ref, send_ref, sem).wait()
 
 
-def attend_kernel(peers, heads, lim_ref, send_ref, q_ref, k_ref, v_ref, out_ref,
-                  recv, qt, vt, top, total, acc, send_sem, recv_sem):
+def attend_kernel(peers, heads, lim_ref, send_ref, q_ref, k_ref, v_ref, w_ref, out_ref, w_pair_ref,
+                  recv, qt, vt, top, total, acc, send_sem, recv_sem, w_sem):
     me = lax.axis_index("req")
     tok = q_ref.shape[0]
     hd = k_ref.shape[1]
@@ -80,6 +80,11 @@
     @pl.loop(1, peers)
     def _(i):
         copy_to(peer_of(peers - i)).start()
+
+    pair_copy = pltpu.make_async_remote_copy(
+        src_ref=w_ref, dst_ref=w_pair_ref, send_sem=w_sem.at[0], recv_sem=w_sem.at[1],
+        device_id={"req": me + 1 - 2 * (me % 2)}, device_id_type=MESH)
+    pair_copy.start()
 
     for h in range(heads):
         cols = slice(h * hd, (h + 1) * hd)
@@ -144,6 +149,137 @@
     @pl.loop(1, peers)
     def _(i):
         copy_to(peer_of(i)).wait_send()
+
+    pair_copy.wait()
+
+
+def project_kernel(far, att_ref, w_ref, w_pair_ref, out_ref,
+                   full, wv, part, got, low, load_sem, send_sem, recv_sem,
+                   part_send, part_recv, out_send, out_recv):
+    me = lax.axis_index("req")
+    head = lax.axis_index("head")
+    hi, lo = me // 2, me % 2
+    half = out_ref.shape[0]
+    columns = w_ref.shape[1]
+    wide = 2 * columns
+
+    def at(z):
+        return {"req": z * 2 + lo}
+
+    load_own = pltpu.make_async_copy(att_ref, full.at[hi], load_sem.at[0])
+    load_w = pltpu.make_async_copy(w_ref, wv.at[lo], load_sem.at[1])
+    load_pair = pltpu.make_async_copy(w_pair_ref, wv.at[1 - lo], load_sem.at[2])
+    load_own.start()
+    load_w.start()
+    load_pair.start()
+
+    barrier = pltpu.get_barrier_semaphore()
+    for k in range(1, far):
+        pl.semaphore_signal(barrier, inc=1, device_id=at(lax.rem(hi + k, far)), device_id_type=MESH)
+    pl.semaphore_signal(barrier, inc=1, device_id={"head": 1 - head}, device_id_type=MESH)
+    pl.semaphore_wait(barrier, far)
+
+    def block_copy(z, to, way):
+        return pltpu.make_async_remote_copy(
+            src_ref=full.at[z], dst_ref=full.at[z], send_sem=send_sem.at[way, z],
+            recv_sem=recv_sem.at[z], device_id=at(to), device_id_type=MESH)
+
+    def part_copy(z):
+        return pltpu.make_async_remote_copy(
+            src_ref=part.at[z, 1 - head], dst_ref=got.at[z], send_sem=part_send.at[z],
+            recv_sem=part_recv.at[z], device_id={"head": 1 - head}, device_id_type=MESH)
+
+    def out_copy(z, owner):
+        return pltpu.make_async_remote_copy(
+            src_ref=low.at[z], dst_ref=out_ref.at[:, pl.ds(pl.multiple_of(owner * wide, wide), wide)],
+            send_sem=out_send.at[z], recv_sem=out_recv.at[owner], device_id=at(z), device_id_type=MESH)
+
+    def compute(z):
+        @pl.loop(0, 2)
+        def _(j):
+            cols = pl.ds(pl.multiple_of(j * columns, columns), columns)
+            terms = jnp.dot(full[z], wv[j], preferred_element_type=jnp.float32)
+            part[z, 0, :, cols] = terms[:half]
+            part[z, 1, :, cols] = terms[half:]
+        part_copy(z).start()
+
+    def finish(z):
+        part_copy(z).wait_recv()
+        rows = (part[z, head] + got[z]).astype(out_ref.dtype)
+
+        @pl.when(z == hi)
+        def _():
+            out_ref[:, pl.ds(pl.multiple_of(hi * wide, wide), wide)] = rows
+
+        @pl.when(z != hi)
+        def _():
+            low[z] = rows
+            out_copy(z, hi).start()
+
+    load_own.wait()
+
+    @pl.when(hi < far - 1)
+    def _():
+        block_copy(hi, hi + 1, 0).start()
+
+    @pl.when(hi > 0)
+    def _():
+        block_copy(hi, hi - 1, 1).start()
+
+    load_w.wait()
+    load_pair.wait()
+    compute(hi)
+
+    @pl.loop(1, far + 1)
+    def _(d):
+        @pl.when((hi - d >= 0) & (d < far))
+        def _():
+            block_copy(hi - d, hi, 0).wait_recv()
+
+            @pl.when(hi < far - 1)
+            def _():
+                block_copy(hi - d, hi + 1, 0).start()
+
+        @pl.when(hi + d < far)
+        def _():
+            block_copy(hi + d, hi, 1).wait_recv()
+
+            @pl.when(hi > 0)
+            def _():
+                block_copy(hi + d, hi - 1, 1).start()
+
+        @pl.loop(0, 2)
+        def _(side):
+            z = hi + d * (2 * side - 1)
+
+            @pl.when((z >= 0) & (z < far))
+            def _():
+                compute(z)
+
+        @pl.loop(0, 2)
+        def _(side):
+            z = hi + (d - 1) * (2 * side - 1)
+
+            @pl.when((z >= 0) & (z < far) & ((d > 1) | (side == 0)))
+            def _():
+                finish(z)
+
+    @pl.loop(0, far)
+    def _(z):
+        @pl.when((z <= hi) & (hi < far - 1))
+        def _():
+            block_copy(z, hi + 1, 0).wait_send()
+
+        @pl.when((z >= hi) & (hi > 0))
+        def _():
+            block_copy(z, hi - 1, 1).wait_send()
+
+        part_copy(z).wait_send()
+
+        @pl.when(z != hi)
+        def _():
+            out_copy(z, hi).wait_send()
+            out_copy(z, z).wait_recv()
 
 
 def local(queries, new_keys, new_values, cluster_kv, cluster_len, piece_slot, cluster_ids, w_out):
@@ -171,11 +307,15 @@
         name="pick",
     )(cluster_ids[:, 0, :], piece_slot, cluster_len, cluster_kv)
     rows = heads * tok
-    attended = pl.pallas_call(
+    any_space = pl.BlockSpec(memory_space=pl.ANY)
+    attended, w_pair = pl.pallas_call(
         functools.partial(attend_kernel, peers, heads),
-        out_shape=jax.ShapeDtypeStruct((tok, heads * hd), jnp.bfloat16),
-        in_specs=[smem, vmem, vmem, vmem, vmem],
-        out_specs=vmem,
+        out_shape=(
+            jax.ShapeDtypeStruct((tok, heads * hd), jnp.bfloat16),
+            jax.ShapeDtypeStruct(w_out.shape, w_out.dtype),
+        ),
+        in_specs=[smem, vmem, vmem, vmem, vmem, any_space],
+        out_specs=(vmem, any_space),
         scratch_shapes=[
             pltpu.VMEM((peers, count, 2, piece_keys, hd), cluster_kv.dtype),
             pltpu.VMEM((hd, rows), jnp.bfloat16),
@@ -185,18 +325,38 @@
             pltpu.VMEM((hd, rows), jnp.float32),
             pltpu.SemaphoreType.DMA((peers,)),
             pltpu.SemaphoreType.DMA((peers,)),
+            pltpu.SemaphoreType.DMA((2,)),
         ],
         compiler_params=pltpu.CompilerParams(
             collective_id=0, has_side_effects=True, vmem_limit_bytes=40 * 2**20),
         name="attend",
-    )(lim, send, queries.reshape(tok, heads * hd), new_keys[:, 0], new_values[:, 0])
-    gathered = lax.all_gather(attended, "req", axis=0, tiled=True)
-    terms = jnp.dot(gathered, w_out, preferred_element_type=jnp.float32)
-    columns = w_out.shape[1]
-    terms = terms.reshape(peers, tok, columns)
-    summed = lax.psum_scatter(terms, "head", scatter_dimension=1, tiled=True).astype(jnp.bfloat16)
-    mine = lax.all_to_all(summed, "req", split_axis=0, concat_axis=0, tiled=True)
-    return jnp.transpose(mine, (1, 0, 2)).reshape(mine.shape[1], peers * columns)
+    )(lim, send, queries.reshape(tok, heads * hd), new_keys[:, 0], new_values[:, 0], w_out)
+    far = peers // 2
+    half = tok // lax.axis_size("head")
+    depth, columns = w_out.shape
+    return pl.pallas_call(
+        functools.partial(project_kernel, far),
+        out_shape=jax.ShapeDtypeStruct((half, peers * columns), jnp.bfloat16),
+        in_specs=[any_space, any_space, any_space],
+        out_specs=vmem,
+        scratch_shapes=[
+            pltpu.VMEM((far, tok, depth), jnp.bfloat16),
+            pltpu.VMEM((2, depth, columns), w_out.dtype),
+            pltpu.VMEM((far, 2, half, 2 * columns), jnp.float32),
+            pltpu.VMEM((far, half, 2 * columns), jnp.float32),
+            pltpu.VMEM((far, half, 2 * columns), jnp.bfloat16),
+            pltpu.SemaphoreType.DMA((3,)),
+            pltpu.SemaphoreType.DMA((2, far)),
+            pltpu.SemaphoreType.DMA((far,)),
+            pltpu.SemaphoreType.DMA((far,)),
+            pltpu.SemaphoreType.DMA((far,)),
+            pltpu.SemaphoreType.DMA((far,)),
+            pltpu.SemaphoreType.DMA((far,)),
+        ],
+        compiler_params=pltpu.CompilerParams(
+            collective_id=1, has_side_effects=True, vmem_limit_bytes=40 * 2**20),
+        name="project",
+    )(attended, w_out, w_pair)
 
 
 def solution(mesh):

time: 278 us -> 206 us (0.74)
  waiting for transfers between devices: 129 us -> 0 us
  Pallas kernels: 100 us -> 200 us
  blocking collectives: 20.1 us -> 0 us
  between operations: 13.5 us -> 0.07 us
  matrix products: 5.83 us -> 0 us
    all_gather x1 -> x0, waiting for transfers between devices: 119 us -> none  [local(): gathered = lax.all_gather(attended, 'req', axis=0, tiled=True)]
    pallas_call x0 -> x1, Pallas kernels: none -> 97.9 us  [local(): pl.pallas_call(functools.partial(project_kernel, far), out_shape=jax.Shap...]
    all_to_all x1 -> x0, blocking collectives: 20.1 us -> none  [local(): lax.all_to_all(summed, 'req', split_axis=0, concat_axis=0, tiled=True)]
    reduce_scatter x1 -> x0, waiting for transfers between devices: 9.72 us -> none  [local(): lax.psum_scatter(terms, 'head', scatter_dimension=1, tiled=True)]
    dot_general x1 -> x0, matrix products: 5.83 us -> none  [local(): terms = jnp.dot(gathered, w_out, preferred_element_type=jnp.float32)]
  transfers between devices with their start and end apart: 2 -> 0, of which waited for: 2 -> 0; matrix products, arithmetic and copies ran while one was open for 0% -> 0% of each run, Pallas kernels for 0% -> 0%
where the time goes in v2:
time: 206 us
  Pallas kernels  200 us (97%)
  local copies, waits for them, and re-layouts  6.34 us (3%)
    pallas_call x1, Pallas kernels, local(): pl.pallas_call(functools.partial(project_kernel, far), out_shape=jax.Shap...  97.9 us
    pallas_call x1, Pallas kernels, local(): pl.pallas_call(functools.partial(attend_kernel, peers, heads), out_shape=...  96.1 us
    pallas_call x1, Pallas kernels, local(): pl.pallas_call(functools.partial(pick_kernel, peers), out_shape=(jax.Shap...  5.54 us
    unnamed x12, local copies, waits for them, and re-layouts  4.85 us

profile of v2, /device:TPU:4, one launch (start us, length us, event | category | flops | bytes accessed | tf_op | source)
XLA Modules:
  0.0 205.9 jit_solution(11217160894212019836)
XLA Ops:
  0.0 0.0 copy-start
  0.0 0.0 copy-start.3
  0.0 0.0 copy-start.2
  0.0 1.5 copy.9.ids_ref
  1.5 1.2 copy.12
  2.7 5.5 %pick.1 = (bf16[8,8,2,128,128]{4,3,2,1,0:T(8,128)(2,1)}, s32[8,8]{1,0:T(8,128)}) custom-call(s32[8,2]{1,0:T(8,128)} %copy.9.ids_ref, s32[16,32]{1,0:T(8,128)} %slot_ref.1, s32[16]{0:T(128)} %len_ref.1, bf16[64,1,2,128,128]{4,3,2,1,0:T(8,128)(2,1)} %kv_ref.1), custom_call_target="tpu_custom_call" | custom-call | tf_op jit(solution)/shard_map/pick/pallas_call | solution.py:294
  8.2 0.0 copy-done
  8.2 0.0 copy-done.3
  8.3 0.0 copy-done.2
  8.3 0.0 copy-start.1
  8.3 2.2 %copy-done.1 = bf16[8,8,2,128,128]{4,3,2,1,0:T(8,128)(2,1)S(1)} copy-done((bf16[8,8,2,128,128]{4,3,2,1,0:T(8,128)(2,1)S(1)}, bf16[8,8,2,128,128]{4,3,2,1,0:T(8,128)(2,1)}, u32[]{:S(2)}) %copy-start.1) | copy-done | bytes 4194328
  10.5 0.0 copy-start.4
  10.5 0.7 copy-done.4
  11.1 96.1 %attend.1 = (bf16[128,2048]{1,0:T(8,128)(2,1)S(1)}, bf16[2048,512]{1,0:T(8,128)(2,1)S(1)}) custom-call(s32[8,8]{1,0:T(8,128)S(1)} %copy-done.4, bf16[8,8,2,128,128]{4,3,2,1,0:T(8,128)(2,1)S(1)} %copy-done.1, bf16[128,2048]{1,0:T(8,128)(2,1)S(1)} %bitcast.7, bf16[128,128]{1,0:T(8,128)(2,1)S(1)} %bitcast.8, bf16[128,128]{1,0:T(8,128)(2,1)S(1)} %bitcast.9, ...), custom_call_target="tpu_custom_call" | custom-call | tf_op jit(solution)/shard_map/attend/pallas_call | solution.py:311
  107.3 97.9 %project.1 = bf16[64,4096]{1,0:T(8,128)(2,1)S(1)} custom-call(bf16[128,2048]{1,0:T(8,128)(2,1)S(1)} %get-tuple-element.11.att_ref, bf16[2048,512]{1,0:T(8,128)(2,1)S(1)} %copy-done, bf16[2048,512]{1,0:T(8,128)(2,1)S(1)} %get-tuple-element.12.w_pair_ref), custom_call_target="tpu_custom_call" | custom-call | tf_op jit(solution)/shard_map/project/pallas_call | solution.py:337
  205.1 0.8 copy.14
Async XLA Ops:
  0.0 8.2 %copy-start = (bf16[2048,512]{1,0:T(8,128)(2,1)S(1)}, bf16[2048,512]{1,0:T(8,128)(2,1)}, u32[]{:S(2)}) copy-start(bf16[2048,512]{1,0:T(8,128)(2,1)} %w_ref.3) | copy-start | bytes 6291460
  0.0 8.2 %copy-start.3 = (bf16[128,1,128]{2,0,1:T(8,128)(2,1)S(1)}, bf16[128,1,128]{2,0,1:T(8,128)(2,1)}, u32[]{:S(2)}) copy-start(bf16[128,1,128]{2,0,1:T(8,128)(2,1)} %param.10) | copy-start | bytes 98308
  0.0 8.3 %copy-start.2 = (bf16[128,1,128]{2,0,1:T(8,128)(2,1)S(1)}, bf16[128,1,128]{2,0,1:T(8,128)(2,1)}, u32[]{:S(2)}) copy-start(bf16[128,1,128]{2,0,1:T(8,128)(2,1)} %param.9) | copy-start | bytes 98308
  8.3 2.2 %copy-start.1 = (bf16[8,8,2,128,128]{4,3,2,1,0:T(8,128)(2,1)S(1)}, bf16[8,8,2,128,128]{4,3,2,1,0:T(8,128)(2,1)}, u32[]{:S(2)}) copy-start(bf16[8,8,2,128,128]{4,3,2,1,0:T(8,128)(2,1)} %get-tuple-element.10.send_ref) | copy-start | bytes 12582916
  10.5 0.7 copy-start.4

commit v3 on v2

--- a/solution.py
+++ b/solution.py
@@ -46,14 +46,16 @@
 
 
 def attend_kernel(peers, heads, lim_ref, send_ref, q_ref, k_ref, v_ref, w_ref, out_ref, w_pair_ref,
-                  recv, qt, vt, top, total, acc, send_sem, recv_sem, w_sem):
+                  recv, qt, top, total, acc, send_sem, recv_sem, w_sem):
     me = lax.axis_index("req")
     tok = q_ref.shape[0]
     hd = k_ref.shape[1]
     count = send_ref.shape[1]
     piece_keys = send_ref.shape[3]
     rows = heads * tok
-    block = min(256, rows)
+    block = min(128, rows)
+    phases = send_sem.shape[1]
+    group = count // phases
     factor = hd ** (-0.5) * LOG2E
 
     barrier = pltpu.get_barrier_semaphore()
@@ -65,21 +67,25 @@
         off = jnp.where(i % 2 == 1, (i + 1) // 2, peers - i // 2)
         return lax.rem(me + off, peers)
 
-    def copy_to(peer):
-        return pltpu.make_async_remote_copy(
-            src_ref=send_ref.at[peer], dst_ref=recv.at[me],
-            send_sem=send_sem.at[peer], recv_sem=recv_sem.at[me],
+    def copy_to(peer, f):
+        part = pl.ds(f * group, group)
+        return pltpu.make_async_remote_copy(
+            src_ref=send_ref.at[peer, part], dst_ref=recv.at[me, part],
+            send_sem=send_sem.at[peer, f], recv_sem=recv_sem.at[me, f],
             device_id={"req": peer}, device_id_type=MESH)
 
-    def copy_from(peer):
-        return pltpu.make_async_remote_copy(
-            src_ref=send_ref.at[peer], dst_ref=recv.at[peer],
-            send_sem=send_sem.at[peer], recv_sem=recv_sem.at[peer],
+    def copy_from(peer, f):
+        part = pl.ds(f * group, group)
+        return pltpu.make_async_remote_copy(
+            src_ref=send_ref.at[peer, part], dst_ref=recv.at[peer, part],
+            send_sem=send_sem.at[peer, f], recv_sem=recv_sem.at[peer, f],
             device_id={"req": peer}, device_id_type=MESH)
 
-    @pl.loop(1, peers)
-    def _(i):
-        copy_to(peer_of(peers - i)).start()
+    @pl.loop(0, phases)
+    def _(f):
+        @pl.loop(1, peers)
+        def _(i):
+            copy_to(peer_of(i), f).start()
 
     pair_copy = pltpu.make_async_remote_copy(
         src_ref=w_ref, dst_ref=w_pair_ref, send_sem=w_sem.at[0], recv_sem=w_sem.at[1],
@@ -104,51 +110,56 @@
         total[:, cols] = jnp.sum(w, axis=0, keepdims=True)
         acc[:, cols] = jnp.dot(own_vt, w.astype(jnp.bfloat16), preferred_element_type=jnp.float32)
 
-    def attend(src_ref, peer):
-        for i in range(count):
-            vt[:, i * piece_keys:(i + 1) * piece_keys] = src_ref[peer, i, 1].T
-
-        @pl.loop(0, rows // block)
-        def _(b):
-            cols = pl.ds(pl.multiple_of(b * block, block), block)
-            q = qt[:, cols]
-            key = lax.broadcasted_iota(jnp.int32, (piece_keys, block), 0)
+    def attend(src_ref, peer, f):
+        keys = group * piece_keys
+        k = src_ref[peer, pl.ds(f * group, group), 0].reshape(keys, hd)
+        vt = jnp.concatenate([src_ref[peer, f * group + i, 1].T for i in range(group)], axis=1)
+        fills = [lim_ref[peer, f * group + i] for i in range(group)]
+        key = lax.broadcasted_iota(jnp.int32, (piece_keys, block), 0)
+
+        def score(b):
+            s = jnp.dot(k, qt[:, b * block:(b + 1) * block], preferred_element_type=jnp.float32)
+            return jnp.concatenate(
+                [jnp.where(key < fills[i], s[i * piece_keys:(i + 1) * piece_keys], NEG) for i in range(group)], axis=0)
+
+        def weigh(b, s):
+            cols = slice(b * block, (b + 1) * block)
             m_old = top[:, cols]
-            m = m_old
-            scores = []
-            for i in range(count):
-                s = jnp.dot(src_ref[peer, i, 0], q, preferred_element_type=jnp.float32)
-                s = jnp.where(key < lim_ref[peer, i], s, NEG)
-                m = jnp.maximum(m, jnp.max(s, axis=0, keepdims=True))
-                scores.append(s)
+            m = jnp.maximum(m_old, jnp.max(s, axis=0, keepdims=True))
             keep = jnp.exp2((m_old - m) * factor)
-            sums = total[:, cols] * keep
-            low = []
-            for s in scores:
-                w = jnp.exp2((s - m) * factor)
-                sums = sums + jnp.sum(w, axis=0, keepdims=True)
-                low.append(w.astype(jnp.bfloat16))
-            mixed = jnp.dot(vt[...], jnp.concatenate(low, axis=0), preferred_element_type=jnp.float32)
+            w = jnp.exp2((s - m) * factor)
+            mixed = jnp.dot(vt, w.astype(jnp.bfloat16), preferred_element_type=jnp.float32)
             top[:, cols] = m
-            total[:, cols] = sums
+            total[:, cols] = total[:, cols] * keep + jnp.sum(w, axis=0, keepdims=True)
             acc[:, cols] = acc[:, cols] * keep + mixed
 
-    attend(send_ref, me)
-
-    @pl.loop(1, peers)
-    def _(i):
-        peer = peer_of(i)
-        copy_from(peer).wait_recv()
-        attend(recv, peer)
+        s = score(0)
+        for b in range(rows // block):
+            ahead = score(b + 1) if b + 1 < rows // block else None
+            weigh(b, s)
+            s = ahead
+
+    @pl.loop(0, phases)
+    def _(f):
+        attend(send_ref, me, f)
+
+    @pl.loop(0, phases * (peers - 1))
+    def _(step):
+        f = step // (peers - 1)
+        peer = peer_of(step % (peers - 1) + 1)
+        copy_from(peer, f).wait_recv()
+        attend(recv, peer, f)
 
     for h in range(heads):
         rows_h = slice(h * tok, (h + 1) * tok)
         o = acc[:, rows_h] / total[:, rows_h]
         out_ref[:, h * hd:(h + 1) * hd] = o.T.astype(out_ref.dtype)
 
-    @pl.loop(1, peers)
-    def _(i):
-        copy_to(peer_of(i)).wait_send()
+    @pl.loop(0, phases)
+    def _(f):
+        @pl.loop(1, peers)
+        def _(i):
+            copy_to(peer_of(i), f).wait_send()
 
     pair_copy.wait()
 
@@ -307,6 +318,7 @@
         name="pick",
     )(cluster_ids[:, 0, :], piece_slot, cluster_len, cluster_kv)
     rows = heads * tok
+    phases = min(4, count)
     any_space = pl.BlockSpec(memory_space=pl.ANY)
     attended, w_pair = pl.pallas_call(
         functools.partial(attend_kernel, peers, heads),
@@ -319,12 +331,11 @@
         scratch_shapes=[
             pltpu.VMEM((peers, count, 2, piece_keys, hd), cluster_kv.dtype),
             pltpu.VMEM((hd, rows), jnp.bfloat16),
-            pltpu.VMEM((hd, count * piece_keys), jnp.bfloat16),
             pltpu.VMEM((1, rows), jnp.float32),
             pltpu.VMEM((1, rows), jnp.float32),
             pltpu.VMEM((hd, rows), jnp.float32),
-            pltpu.SemaphoreType.DMA((peers,)),
-            pltpu.SemaphoreType.DMA((peers,)),
+            pltpu.SemaphoreType.DMA((peers, phases)),
+            pltpu.SemaphoreType.DMA((peers, phases)),
             pltpu.SemaphoreType.DMA((2,)),
         ],
         compiler_params=pltpu.CompilerParams(

time: 206 us -> 162 us (0.79); the launches traced: 206 us -> 160 us
  Pallas kernels: 200 us -> 153 us
    pallas_call x1, Pallas kernels: 97.9 us -> 48.9 us  [local(): pl.pallas_call(functools.partial(project_kernel, far), out_shape=jax.Shap...]
    pallas_call x1, Pallas kernels: 96.1 us -> 98.8 us  [local(): pl.pallas_call(functools.partial(attend_kernel, peers, heads), out_shape=...]
where the time goes in v3:
time: 162 us; the launch traced here: 160 us
  Pallas kernels  153 us (94%)
  local copies, waits for them, and re-layouts  6.34 us (4%)
    pallas_call x1, Pallas kernels, local(): pl.pallas_call(functools.partial(attend_kernel, peers, heads), out_shape=...  98.8 us
    pallas_call x1, Pallas kernels, local(): pl.pallas_call(functools.partial(project_kernel, far), out_shape=jax.Shap...  48.9 us
    pallas_call x1, Pallas kernels, local(): pl.pallas_call(functools.partial(pick_kernel, peers), out_shape=(jax.Shap...  5.54 us
    unnamed x12, local copies, waits for them, and re-layouts  4.85 us

profile of v3, /device:TPU:4, one launch (start us, length us, event | category | flops | bytes accessed | tf_op | source)
XLA Modules:
  0.0 159.7 jit_solution(4725201774043947319)
XLA Ops:
  0.0 0.0 copy-start
  0.0 0.0 copy-start.3
  0.0 0.0 copy-start.2
  0.0 1.5 copy.9.ids_ref
  1.5 1.2 copy.12
  2.7 5.5 %pick.1 = (bf16[8,8,2,128,128]{4,3,2,1,0:T(8,128)(2,1)}, s32[8,8]{1,0:T(8,128)}) custom-call(s32[8,2]{1,0:T(8,128)} %copy.9.ids_ref, s32[16,32]{1,0:T(8,128)} %slot_ref.1, s32[16]{0:T(128)} %len_ref.1, bf16[64,1,2,128,128]{4,3,2,1,0:T(8,128)(2,1)} %kv_ref.1), custom_call_target="tpu_custom_call" | custom-call | tf_op jit(solution)/shard_map/pick/pallas_call | solution.py:305
  8.2 0.0 copy-done
  8.2 0.0 copy-done.3
  8.3 0.0 copy-done.2
  8.3 0.0 copy-start.1
  8.3 2.2 %copy-done.1 = bf16[8,8,2,128,128]{4,3,2,1,0:T(8,128)(2,1)S(1)} copy-done((bf16[8,8,2,128,128]{4,3,2,1,0:T(8,128)(2,1)S(1)}, bf16[8,8,2,128,128]{4,3,2,1,0:T(8,128)(2,1)}, u32[]{:S(2)}) %copy-start.1) | copy-done | bytes 4194328
  10.5 0.0 copy-start.4
  10.5 0.7 copy-done.4
  11.1 98.8 %attend.1 = (bf16[128,2048]{1,0:T(8,128)(2,1)S(1)}, bf16[2048,512]{1,0:T(8,128)(2,1)S(1)}) custom-call(s32[8,8]{1,0:T(8,128)S(1)} %copy-done.4, bf16[8,8,2,128,128]{4,3,2,1,0:T(8,128)(2,1)S(1)} %copy-done.1, bf16[128,2048]{1,0:T(8,128)(2,1)S(1)} %bitcast.7, bf16[128,128]{1,0:T(8,128)(2,1)S(1)} %bitcast.8, bf16[128,128]{1,0:T(8,128)(2,1)S(1)} %bitcast.9, ...), custom_call_target="tpu_custom_call" | custom-call | tf_op jit(solution)/shard_map/attend/pallas_call | solution.py:323
  110.0 48.9 %project.1 = bf16[64,4096]{1,0:T(8,128)(2,1)S(1)} custom-call(bf16[128,2048]{1,0:T(8,128)(2,1)S(1)} %get-tuple-element.11.att_ref, bf16[2048,512]{1,0:T(8,128)(2,1)S(1)} %copy-done, bf16[2048,512]{1,0:T(8,128)(2,1)S(1)} %get-tuple-element.12.w_pair_ref), custom_call_target="tpu_custom_call" | custom-call | tf_op jit(solution)/shard_map/project/pallas_call | solution.py:348
  158.9 0.8 copy.14
Async XLA Ops:
  0.0 8.2 %copy-start = (bf16[2048,512]{1,0:T(8,128)(2,1)S(1)}, bf16[2048,512]{1,0:T(8,128)(2,1)}, u32[]{:S(2)}) copy-start(bf16[2048,512]{1,0:T(8,128)(2,1)} %w_ref.3) | copy-start | bytes 6291460
  0.0 8.2 %copy-start.3 = (bf16[128,1,128]{2,0,1:T(8,128)(2,1)S(1)}, bf16[128,1,128]{2,0,1:T(8,128)(2,1)}, u32[]{:S(2)}) copy-start(bf16[128,1,128]{2,0,1:T(8,128)(2,1)} %param.10) | copy-start | bytes 98308
  0.0 8.3 %copy-start.2 = (bf16[128,1,128]{2,0,1:T(8,128)(2,1)S(1)}, bf16[128,1,128]{2,0,1:T(8,128)(2,1)}, u32[]{:S(2)}) copy-start(bf16[128,1,128]{2,0,1:T(8,128)(2,1)} %param.9) | copy-start | bytes 98308
  8.3 2.2 %copy-start.1 = (bf16[8,8,2,128,128]{4,3,2,1,0:T(8,128)(2,1)S(1)}, bf16[8,8,2,128,128]{4,3,2,1,0:T(8,128)(2,1)}, u32[]{:S(2)}) copy-start(bf16[8,8,2,128,128]{4,3,2,1,0:T(8,128)(2,1)} %get-tuple-element.10.send_ref) | copy-start | bytes 12582916
  10.5 0.7 copy-start.4

commit v4 on v3

--- a/solution.py
+++ b/solution.py
@@ -12,10 +12,10 @@
 LOG2E = 1.4426950408889634
 
 
-def pick_kernel(peers, ids_ref, slot_ref, len_ref, kv_ref, send_ref, lim_ref, pick, count, sem):
+def pick_kernel(peers, ids_ref, slot_ref, len_ref, kv_ref, send_ref, lim_ref, pick, count, held_pieces, in_sem, out_sem):
     me = lax.axis_index("req")
     held, _, _, piece_keys, _ = kv_ref.shape
-    sel = ids_ref.shape[1]
+    sel = ids_ref.shape[2]
     pieces = slot_ref.shape[1]
     per = pieces // peers
     base = me * held
@@ -23,17 +23,17 @@
     @pl.loop(0, peers)
     def _(r):
         for s in range(sel):
-            c = ids_ref[r, s]
+            c = ids_ref[r, 0, s]
             n = jnp.int32(0)
             for p in range(pieces):
                 loc = slot_ref[c, p] - base
                 pick[n] = loc
                 n = n + ((loc >= 0) & (loc < held)).astype(jnp.int32)
             for j in range(per):
-                pltpu.make_async_copy(kv_ref.at[pick[j], 0], send_ref.at[r, s * per + j], sem).start()
+                pltpu.make_async_copy(kv_ref.at[pick[j], 0], held_pieces.at[r, s * per + j], in_sem.at[r]).start()
 
     for s in range(sel):
-        c = ids_ref[me, s]
+        c = ids_ref[me, 0, s]
         fill = len_ref[c]
         for o in range(peers):
             count[o] = 0
@@ -42,11 +42,22 @@
             j = count[o]
             lim_ref[o, s * per + j] = fill - p * piece_keys
             count[o] = j + 1
-    pltpu.make_async_copy(send_ref, send_ref, sem).wait()
+
+    def put(r):
+        return pltpu.make_async_copy(held_pieces.at[r], send_ref.at[r], out_sem.at[r])
+
+    @pl.loop(0, peers)
+    def _(r):
+        pltpu.make_async_copy(send_ref.at[r], held_pieces.at[r], in_sem.at[r]).wait()
+        put(r).start()
+
+    @pl.loop(0, peers)
+    def _(r):
+        put(r).wait()
 
 
 def attend_kernel(peers, heads, lim_ref, send_ref, q_ref, k_ref, v_ref, w_ref, out_ref, w_pair_ref,
-                  recv, qt, top, total, acc, send_sem, recv_sem, w_sem):
+                  recv, qt, top, total, acc, send_sem, recv_sem, w_sem, own_sem):
     me = lax.axis_index("req")
     tok = q_ref.shape[0]
     hd = k_ref.shape[1]
@@ -58,6 +69,8 @@
     group = count // phases
     factor = hd ** (-0.5) * LOG2E
 
+    own_copy = pltpu.make_async_copy(send_ref.at[me], recv.at[me], own_sem)
+    own_copy.start()
     barrier = pltpu.get_barrier_semaphore()
     for k in range(1, peers):
         pl.semaphore_signal(barrier, inc=1, device_id={"req": lax.rem(me + k, peers)}, device_id_type=MESH)
@@ -93,8 +106,7 @@
     pair_copy.start()
 
     for h in range(heads):
-        cols = slice(h * hd, (h + 1) * hd)
-        qt[:, h * tok:(h + 1) * tok] = q_ref[:, cols].T
+        qt[:, h * tok:(h + 1) * tok] = q_ref[:, h, :].T
     own_vt = v_ref[...].T
 
     @pl.loop(0, rows // block)
@@ -139,9 +151,11 @@
             weigh(b, s)
             s = ahead
 
+    own_copy.wait()
+
     @pl.loop(0, phases)
     def _(f):
-        attend(send_ref, me, f)
+        attend(recv, me, f)
 
     @pl.loop(0, phases * (peers - 1))
     def _(step):
@@ -302,31 +316,33 @@
     count = sel * (pieces // peers)
     vmem = pl.BlockSpec(memory_space=pltpu.VMEM)
     smem = pl.BlockSpec(memory_space=pltpu.SMEM)
+    any_space = pl.BlockSpec(memory_space=pltpu.HBM)
     send, lim = pl.pallas_call(
         functools.partial(pick_kernel, peers),
         out_shape=(
             jax.ShapeDtypeStruct((peers, count, 2, piece_keys, hd), cluster_kv.dtype),
             jax.ShapeDtypeStruct((peers, count), jnp.int32),
         ),
-        in_specs=[smem, smem, smem, pl.BlockSpec(memory_space=pl.ANY)],
-        out_specs=(vmem, smem),
+        in_specs=[smem, smem, smem, any_space],
+        out_specs=(any_space, smem),
         scratch_shapes=[
             pltpu.SMEM((pieces + 1,), jnp.int32),
             pltpu.SMEM((peers,), jnp.int32),
-            pltpu.SemaphoreType.DMA,
+            pltpu.VMEM((peers, count, 2, piece_keys, hd), cluster_kv.dtype),
+            pltpu.SemaphoreType.DMA((peers,)),
+            pltpu.SemaphoreType.DMA((peers,)),
         ],
         name="pick",
-    )(cluster_ids[:, 0, :], piece_slot, cluster_len, cluster_kv)
+    )(cluster_ids, piece_slot, cluster_len, cluster_kv)
     rows = heads * tok
     phases = min(4, count)
-    any_space = pl.BlockSpec(memory_space=pl.ANY)
     attended, w_pair = pl.pallas_call(
         functools.partial(attend_kernel, peers, heads),
         out_shape=(
             jax.ShapeDtypeStruct((tok, heads * hd), jnp.bfloat16),
             jax.ShapeDtypeStruct(w_out.shape, w_out.dtype),
         ),
-        in_specs=[smem, vmem, vmem, vmem, vmem, any_space],
+        in_specs=[smem, any_space, vmem, vmem, vmem, any_space],
         out_specs=(vmem, any_space),
         scratch_shapes=[
             pltpu.VMEM((peers, count, 2, piece_keys, hd), cluster_kv.dtype),
@@ -337,11 +353,12 @@
             pltpu.SemaphoreType.DMA((peers, phases)),
             pltpu.SemaphoreType.DMA((peers, phases)),
             pltpu.SemaphoreType.DMA((2,)),
+            pltpu.SemaphoreType.DMA,
         ],
         compiler_params=pltpu.CompilerParams(
-            collective_id=0, has_side_effects=True, vmem_limit_bytes=40 * 2**20),
+            collective_id=0, has_side_effects=True, vmem_limit_bytes=60 * 2**20),
         name="attend",
-    )(lim, send, queries.reshape(tok, heads * hd), new_keys[:, 0], new_values[:, 0], w_out)
+    )(lim, send, queries, new_keys[:, 0], new_values[:, 0], w_out)
     far = peers // 2
     half = tok // lax.axis_size("head")
     depth, columns = w_out.shape
@@ -365,7 +382,7 @@
             pltpu.SemaphoreType.DMA((far,)),
         ],
         compiler_params=pltpu.CompilerParams(
-            collective_id=1, has_side_effects=True, vmem_limit_bytes=40 * 2**20),
+            collective_id=1, has_side_effects=True, vmem_limit_bytes=60 * 2**20),
         name="project",
     )(attended, w_out, w_pair)
 

time: 162 us -> 161 us (level)
  local copies, waits for them, and re-layouts: 6.34 us -> 3.21 us
  Pallas kernels: 153 us -> 155 us
    unnamed x12 -> x2, local copies, waits for them, and re-layouts: 4.85 us -> 3.21 us
where the time goes in v4:
time: 161 us; the launch traced here: 159 us
  Pallas kernels  155 us (96%)
  local copies, waits for them, and re-layouts  3.21 us (2%)
    pallas_call x1, Pallas kernels, local(): pl.pallas_call(functools.partial(attend_kernel, peers, heads), out_shape=...  100 us
    pallas_call x1, Pallas kernels, local(): pl.pallas_call(functools.partial(project_kernel, far), out_shape=jax.Shap...  49.4 us
    pallas_call x1, Pallas kernels, local(): pl.pallas_call(functools.partial(pick_kernel, peers), out_shape=(jax.Shap...  5.74 us

profile of v4, /device:TPU:4, one launch (start us, length us, event | category | flops | bytes accessed | tf_op | source)
XLA Modules:
  0.0 158.7 jit_solution(17511023393083701561)
XLA Ops:
  0.0 1.3 copy.9.ids_ref
  1.3 5.7 %pick.1 = (bf16[8,8,2,128,128]{4,3,2,1,0:T(8,128)(2,1)}, s32[8,8]{1,0:T(8,128)}) custom-call(s32[8,1,2]{2,1,0:T(1,128)} %copy.9.ids_ref, s32[16,32]{1,0:T(8,128)} %slot_ref.1, s32[16]{0:T(128)} %len_ref.1, bf16[64,1,2,128,128]{4,3,2,1,0:T(8,128)(2,1)} %kv_ref.1), custom_call_target="tpu_custom_call" | custom-call | tf_op jit(solution)/shard_map/pick/pallas_call | solution.py:320
  7.1 100.3 %attend.1 = (bf16[128,2048]{1,0:T(8,128)(2,1)}, bf16[2048,512]{1,0:T(8,128)(2,1)}) custom-call(s32[8,8]{1,0:T(8,128)} %get-tuple-element.9.lim_ref, bf16[8,8,2,128,128]{4,3,2,1,0:T(8,128)(2,1)} %get-tuple-element.10.send_ref, bf16[128,16,128]{2,1,0:T(8,128)(2,1)} %q_ref.1, bf16[128,128]{1,0:T(8,128)(2,1)} %bitcast.2, bf16[128,128]{1,0:T(8,128)(2,1)} %bitcast.3, ...), custom_call_target="tpu_custom_call" | custom-call | tf_op jit(solution)/shard_map/attend/pallas_call | solution.py:339
  107.4 49.4 %project.1 = bf16[64,4096]{1,0:T(8,128)(2,1)} custom-call(bf16[128,2048]{1,0:T(8,128)(2,1)} %get-tuple-element.11.att_ref, bf16[2048,512]{1,0:T(8,128)(2,1)} %w_ref.3, bf16[2048,512]{1,0:T(8,128)(2,1)} %get-tuple-element.12.w_pair_ref), custom_call_target="tpu_custom_call" | custom-call | tf_op jit(solution)/shard_map/project/pallas_call | solution.py:365
  156.8 1.9 %copy.11 = bf16[64,4096]{1,0:T(8,128)(2,1)} copy(bf16[64,4096]{1,0:T(8,128)(2,1)} %project.1) | data formatting | bytes 1048576
